TPU v7x, 32 devices: a whole 2x2x4 slice. The times are simulated.
32 devices in a mesh: blk: 2 (over x), grid: 16 (over z, y, core).
Axes of the slice: x: 2, y: 2, z: 4, core: 2. Of those that a mesh axis runs over, the one named last changes fastest.
Arguments:
- centers: bfloat16 [4096, 512], P(('blk', 'grid')), as said below
- weights: float32 [4096, 1000], P(('blk', 'grid')), may hold values from -6 to 6
- batch_index: int32 [512], replicated, may hold values from 0 to 4095, as said below
- labels: int32 [512], replicated, may hold values from 0 to 999
- sub_index: int32 [256], P(('blk', 'grid')), may hold values from 0 to 127
- eigvecs: bfloat16 [256, 160], P(('blk', 'grid')), may hold values from -0.375 to 0.375
- scales: float32 [160], replicated, may hold values from 1 to 16
Outputs:
- predictions: bfloat16 [512, 1000], replicated
- center_grad: bfloat16 [4096, 1000], P(('blk', 'grid'))
- sub_increment: float32 [256, 1000], P(('blk', 'grid'))
Inputs may be any that keep to these rules, and one draw needn't show every extreme that they name: Each device's block of 128 centers is named by exactly 512 / 32 entries of batch_index. sub_index: entry i names center (i // 8) * 128 + sub_index[i]. centers: row scales of order one.
All inputs are finite; a program needn't handle non-finite values.
Results may differ from a plain program's by a relative error of at most 0.0011.
The roundings to bfloat16 on the way count: a program that leaves them out, or rounds other values in their place, can miss the bound.
Values may be sent and summed in bfloat16 or wider, within the bound.
A program may use at most 64 MiB of HBM per device.

v0:
```python
import jax
import jax.numpy as jnp
from jax import lax
from jax.sharding import PartitionSpec as P

SOFTEN = 1.0
SPREAD = 4.0


def kernel(left, right):
    left_sq = jnp.sum(jnp.square(left.astype(jnp.float32)), axis=1)
    right_sq = jnp.sum(jnp.square(right.astype(jnp.float32)), axis=1)
    cross = lax.dot_general(
        left, right, (((1,), (1,)), ((), ())), preferred_element_type=jnp.float32
    )
    dist = jnp.sqrt(jnp.maximum(left_sq[:, None] + right_sq[None, :] - 2.0 * cross, 0.0) + SOFTEN)
    return jnp.exp(-dist / SPREAD)


def one_hot(label_rows, classes):
    return (label_rows[:, None] == jnp.arange(classes, dtype=jnp.int32)[None, :]).astype(
        jnp.float32
    )


def local(centers, weights, batch_index, labels, sub_index, eigvecs, scales):
    myself = lax.axis_index(("blk", "grid"))
    held = centers.shape[0]
    classes = weights.shape[1]
    owner = batch_index // held
    within = batch_index % held
    picked = jnp.take(centers, within, axis=0).astype(jnp.float32)
    picked = jnp.where((owner == myself)[:, None], picked, 0.0)
    batch = lax.psum(picked, ("blk", "grid")).astype(jnp.bfloat16)
    kbz = kernel(batch, centers).astype(jnp.bfloat16)
    partial_out = jnp.dot(kbz, weights.astype(jnp.bfloat16), preferred_element_type=jnp.float32)
    total = lax.psum(partial_out, ("blk", "grid"))
    predictions = total.astype(jnp.bfloat16)
    resid = (total - one_hot(labels, classes)).astype(jnp.bfloat16)
    subset_here = jnp.take(centers, sub_index, axis=0)
    sub_rows = lax.all_gather(subset_here, ("blk", "grid"), axis=0, tiled=True)
    vec_rows = lax.all_gather(eigvecs, ("blk", "grid"), axis=0, tiled=True)
    kzs = kernel(centers, sub_rows).astype(jnp.bfloat16)
    ksb_piece = kernel(sub_rows, batch).astype(jnp.bfloat16)
    kze_next = jnp.dot(kzs, vec_rows, preferred_element_type=jnp.float32)
    proj_next = lax.dot_general(
        vec_rows, ksb_piece, (((0,), (0,)), ((), ())), preferred_element_type=jnp.float32
    )
    coeff = jnp.dot(proj_next, resid.astype(jnp.float32), precision=lax.Precision.HIGHEST)
    scaled = scales[:, None] * coeff
    sub_increment = jnp.dot(eigvecs.astype(jnp.float32), scaled, precision=lax.Precision.HIGHEST)
    correction = jnp.dot(kze_next, scaled, precision=lax.Precision.HIGHEST)
    first = lax.dot_general(
        kbz, resid, (((0,), (0,)), ((), ())), preferred_element_type=jnp.float32
    )
    center_grad = (first - correction).astype(jnp.bfloat16)
    return (predictions, center_grad, sub_increment)


def solution(mesh):
    return jax.shard_map(
        local,
        mesh=mesh,
        in_specs=(
            P(("blk", "grid"), None),
            P(("blk", "grid"), None),
            P(),
            P(),
            P(("blk", "grid")),
            P(("blk", "grid"), None),
            P(),
        ),
        out_specs=(P(), P(("blk", "grid"), None), P(("blk", "grid"), None)),
        check_vma=False,
    )
```

profile of v0, /device:TPU:1, one launch (start us, length us, event | category | flops | bytes accessed | tf_op | source)
XLA Modules:
  0.0 213.7 jit_solution(7999707913510482286)
XLA Ops:
  7.2 0.0 all-reduce.3.cloned.1.call-start
  7.2 1.0 multiply_reduce_fusion.2
  8.3 0.7 compare_and_fusion.1
  9.0 2.0 gather_fusion
  11.0 0.2 convert_select_fusion
  11.2 50.7 %all-reduce.4 = bf16[512,512]{1,0:T(8,128)(2,1)S(1)} all-reduce(f32[512,512]{1,0:T(8,128)S(1)} %convert_select_fusion), channel_id=1, replica_groups=mesh['blk'=2,'grid'=16] {'blk','grid'}, use_global_device_ids=true, to_apply=%region_0.1 | all-reduce | flops 262144 | bytes 1572864 | tf_op jit(solution)/shard_map/psum | solution.py:34
  61.9 0.2 multiply_reduce_fusion
  62.1 0.3 fusion.17
  62.4 0.0 copy-start.3
  62.5 1.7 fusion.35
  64.2 0.0 all-reduce.3.cloned.1.call-update
  64.3 0.6 gather_fusion.1
  64.9 42.0 %all_gather.7 = bf16[256,160]{1,0:T(8,128)(2,1)S(1)} all-gather(bf16[8,160]{1,0:T(8,128)(2,1)S(1)} %copy-done.3), channel_id=1, replica_groups=mesh['blk'=2,'grid'=16] {'blk','grid'}, dimensions={0}, use_global_device_ids=true | all-gather | bytes 84480 | tf_op jit(solution)/shard_map/all_gather | solution.py:42
  106.9 0.1 broadcast_select_fusion
  106.9 37.3 %all_gather.6 = bf16[256,512]{1,0:T(8,128)(2,1)S(1)} all-gather(bf16[8,512]{1,0:T(8,128)(2,1)S(1)} %broadcast_select_fusion), channel_id=1, replica_groups=mesh['blk'=2,'grid'=16] {'blk','grid'}, dimensions={0}, use_global_device_ids=true | all-gather | bytes 270336 | tf_op jit(solution)/shard_map/all_gather | solution.py:41
  144.3 0.1 multiply_reduce_fusion.1
  144.4 0.4 fusion.27
  144.8 0.7 fusion.9
  145.5 52.8 %all-reduce.3.cloned.1.call-done = f32[512,1000]{0,1:T(8,128)} async-done(((f32[512,1000]{0,1:T(8,128)}), f32[512,1000]{0,1:T(8,128)}) %all-reduce.3.cloned.1.call-update) | async-done | bytes 2048016 | tf_op jit(solution)/shard_map/psum | solution.py:37
  198.3 3.6 %convolution_multiply_fusion = f32[160,1000]{1,0:T(8,128)S(1)} fusion(f32[512,160]{1,0:T(8,128)S(1)} %fusion.9, f32[160]{0:T(256)S(1)} %copy-done.5, f32[512,1000]{0,1:T(8,128)} %all-reduce.3.cloned.1.call-done, s32[512]{0:T(512)S(1)} %copy-done.4), kind=kOutput, calls=%fused_computation.4 | convolution fusion | flops 985248000 | bytes 3018368 | tf_op jit(solution)/shard_map/dot_general | solution.py:49
  201.9 0.9 convolution_bitcast_fusion
  202.8 1.8 fusion.57
  204.7 1.1 convert_element_type.50
  205.8 1.1 fusion.8
  (17 shorter events, 0.1 us)
Async XLA Ops:
  7.2 1.8 copy-start
  7.2 191.1 %all-reduce.3.cloned.1.call-start = ((), (), s32[]{:S(2)}) async-start(), calls=%async_computation | async-start | bytes 4096000 | tf_op jit(solution)/shard_map/psum | solution.py:37
  11.2 51.3 %copy-start.2 = (f32[128,1000]{0,1:T(8,128)S(1)}, f32[128,1000]{0,1:T(8,128)}, u32[]{:S(2)}) copy-start(f32[128,1000]{0,1:T(8,128)} %param.8) | copy-start | bytes 1536004
  62.4 1.8 copy-start.6
  62.4 2.4 %copy-start.3 = (bf16[8,160]{1,0:T(8,128)(2,1)S(1)}, bf16[8,160]{1,0:T(8,128)(2,1)}, u32[]{:S(2)}) copy-start(bf16[8,160]{1,0:T(8,128)(2,1)} %param.12) | copy-start | bytes 7684
  64.2 134.0 %copy-start.4 = (s32[512]{0:T(512)S(1)}, s32[512]{0:T(512)}, u32[]{:S(2)}) copy-start(s32[512]{0:T(512)} %param.10) | copy-start | bytes 6148
  64.3 134.0 %copy-start.5 = (f32[160]{0:T(256)S(1)}, f32[160]{0:T(256)}, u32[]{:S(2)}) copy-start(f32[160]{0:T(256)} %param.13) | copy-start | bytes 1924
  198.3 6.4 %copy-start.1 = (f32[512,1000]{0,1:T(8,128)S(1)}, f32[512,1000]{0,1:T(8,128)}, u32[]{:S(2)}) copy-start(f32[512,1000]{0,1:T(8,128)} %all-reduce.3.cloned.1.call-done) | copy-start | bytes 6144004
Sparse Core Ops, SparseCore 0:
  64.4 133.8 all-reduce.2
where the time goes:
time: 215 us; the launch traced here: 214 us
  blocking collectives  130 us (60%)
  waiting for transfers between devices  52.8 us (25%)
  between operations  14.2 us (7%)
  matrix products  10.6 us (5%)
  other arithmetic  3.42 us (2%)
  local copies, waits for them, and re-layouts  2.58 us (1%)
    psum x1, waiting for transfers between devices, local(): total = lax.psum(partial_out, ('blk', 'grid'))  52.8 us
    psum x1, blocking collectives, local(): batch = lax.psum(picked, ('blk', 'grid')).astype(jnp.bfloat16)  50.7 us
    all_gather x1, blocking collectives, local(): vec_rows = lax.all_gather(eigvecs, ('blk', 'grid'), axis=0, tiled=True)  42 us
    all_gather x1, blocking collectives, local(): sub_rows = lax.all_gather(subset_here, ('blk', 'grid'), axis=0, tiled=True)  37.3 us
  transfers between devices with their start and end apart: 1, of which 1 were waited for; matrix products, arithmetic and copies ran while one was open for 1% of the time, Pallas kernels for 0%

commit v1 on v0

--- a/solution.py
+++ b/solution.py
@@ -1,10 +1,19 @@
+import functools
+
 import jax
 import jax.numpy as jnp
 from jax import lax
+from jax.experimental import pallas as pl
+from jax.experimental.pallas import tpu as pltpu
 from jax.sharding import PartitionSpec as P
 
 SOFTEN = 1.0
 SPREAD = 4.0
+CORES = 2
+MESH = pl.DeviceIdType.MESH
+F32 = jnp.float32
+BF16 = jnp.bfloat16
+HIGHEST = lax.Precision.HIGHEST
 
 
 def kernel(left, right):
@@ -57,9 +66,334 @@
     return (predictions, center_grad, sub_increment)
 
 
+def iota(shape, dim):
+    return lax.broadcasted_iota(jnp.int32, shape, dim)
+
+
+def to_col(row, n):
+    return jnp.sum(jnp.where(iota((n, n), 0) == iota((n, n), 1), row, 0.0), axis=1, keepdims=True)
+
+
+def to_row(col, n):
+    return jnp.sum(jnp.where(iota((n, n), 0) == iota((n, n), 1), col, 0.0), axis=0, keepdims=True)
+
+
+def hot(mask):
+    return jnp.where(mask, 1.0, 0.0).astype(BF16)
+
+
+def nn(a, b, **kw):
+    return jnp.dot(a, b, preferred_element_type=F32, **kw)
+
+
+def nt(a, b):
+    return lax.dot_general(a, b, (((1,), (1,)), ((), ())), preferred_element_type=F32)
+
+
+def tn(a, b):
+    return lax.dot_general(a, b, (((0,), (0,)), ((), ())), preferred_element_type=F32)
+
+
+def sq_col(rows):
+    return jnp.sum(jnp.square(rows.astype(F32)), axis=1, keepdims=True)
+
+
+def kern(left, right, left_sq, right_sq):
+    dist = jnp.sqrt(jnp.maximum(left_sq + right_sq - 2.0 * nt(left, right), 0.0) + SOFTEN)
+    return jnp.exp(-dist / SPREAD).astype(BF16)
+
+
+def body(
+    n_grid, chips, share, classes,
+    centers, weights, batch_index, labels, sub_index, eigvecs, scales,
+    pred_out, grad_out, sub_out,
+    csib, wts, wsib, gath, gath2, batch, part, recv, pred, left, resid,
+    c_sem, w_sem, g_send, g_fwd, g_recv, h_send, h_fwd, h_recv,
+    p_send, p_fwd, p_recv, r_send, r_recv,
+):
+    held, width = centers.shape
+    rows_b = batch_index.shape[1]
+    cp = wts.shape[1]
+    sub_dev, rank = eigvecs.shape
+    n = chips * CORES
+    subset = n * sub_dev
+    half = rows_b // CORES
+    me = lax.axis_index("blk") * n_grid + lax.axis_index("grid")
+    chip, core = me // CORES, lax.rem(me, CORES)
+
+    def at(dev):
+        return (dev // n_grid, lax.rem(dev, n_grid))
+
+    sib = chip * CORES + (1 - core)
+
+    def peer_chip(k):
+        return lax.rem(chip + k, chips)
+
+    def from_chip(k):
+        return lax.rem(chip + chips - k, chips)
+
+    barrier = pltpu.get_barrier_semaphore()
+
+    def greet(k, carry):
+        pl.semaphore_signal(
+            barrier, inc=1, device_id=at(peer_chip(k) * CORES + core), device_id_type=MESH
+        )
+        return carry
+
+    pl.semaphore_signal(barrier, inc=1, device_id=at(sib), device_id_type=MESH)
+    lax.fori_loop(1, chips, greet, 0)
+
+    wts[...] = jnp.zeros_like(wts)
+    wts[:, :classes] = weights[...].astype(BF16)
+
+    bi_row = batch_index[...].astype(F32)
+    bi_col = to_col(bi_row, rows_b)
+    own_row = jnp.floor((bi_row + 0.5) * (1.0 / held))
+    own_col = jnp.floor((bi_col + 0.5) * (1.0 / held))
+    r_i, c_i = iota((rows_b, rows_b), 0), iota((rows_b, rows_b), 1)
+    same = own_col == own_row
+    rank_row = jnp.sum(jnp.where(same, jnp.where(r_i < c_i, 1.0, 0.0), 0.0), axis=0, keepdims=True)
+    rank_col = jnp.sum(jnp.where(same, jnp.where(c_i < r_i, 1.0, 0.0), 0.0), axis=1, keepdims=True)
+    pos_row = own_row * share + rank_row
+    pos_col = own_col * share + rank_col
+    mine = (iota((share, rows_b), 0) + me * share).astype(F32)
+    within = bi_col - own_col * held
+    pick = hot(within == iota((rows_b, held), 1).astype(F32))
+    sel = nn(hot(mine == pos_row), pick).astype(BF16)
+    gath[me] = nn(sel, centers[...]).astype(BF16)
+
+    pair = 2 * sub_dev
+    sub_col = jnp.sum(
+        jnp.where(
+            iota((pair, sub_dev), 0) == iota((pair, sub_dev), 1),
+            sub_index[...].astype(F32), 0.0,
+        ),
+        axis=1, keepdims=True,
+    )
+    sub_hot = hot(
+        (iota((pair, held), 0) < sub_dev) & (sub_col == iota((pair, held), 1).astype(F32))
+    )
+    eig16 = nn(
+        hot(iota((pair, sub_dev), 0) == iota((pair, sub_dev), 1) + sub_dev), eigvecs[...]
+    ).astype(BF16)
+    eig16 = nn(eig16, hot(iota((rank, width), 0) == iota((rank, width), 1)))
+    gath2[me] = (nn(sub_hot, centers[...]) + eig16).astype(BF16)
+
+    pl.semaphore_wait(barrier, chips)
+
+    def send(src, dst, s_sem, r_sem, dev):
+        return pltpu.make_async_remote_copy(
+            src_ref=src, dst_ref=dst, send_sem=s_sem, recv_sem=r_sem,
+            device_id=at(dev), device_id_type=MESH,
+        )
+
+    def gather_start(buf, slot, s_sem, f_sem, r_sem):
+        def go(k, carry):
+            q = peer_chip(k)
+            send(buf.at[slot(me)], buf.at[slot(me)], s_sem.at[q], r_sem.at[me],
+                 q * CORES + core).start()
+            return carry
+
+        lax.fori_loop(1, chips, go, 0)
+        send(buf.at[slot(me)], buf.at[slot(me)], f_sem.at[chip], r_sem.at[me], sib).start()
+
+    def gather_pass(buf, slot, f_sem, r_sem):
+        def go(k, carry):
+            q = from_chip(k)
+            dev = q * CORES + core
+            here = buf.at[slot(dev)]
+            send(here, here, f_sem.at[q], r_sem.at[dev], sib).wait_recv()
+            send(here, here, f_sem.at[q], r_sem.at[dev], sib).start()
+            return carry
+
+        lax.fori_loop(1, chips, go, 0)
+
+    def gather_rest(buf, slot, f_sem, r_sem):
+        def go(q, carry):
+            dev = q * CORES + (1 - core)
+            here = buf.at[slot(dev)]
+            send(here, here, f_sem.at[q], r_sem.at[dev], sib).wait_recv()
+            return carry
+
+        lax.fori_loop(0, chips, go, 0)
+
+    def gather_end(buf, slot, s_sem, f_sem, r_sem):
+        def go(k, carry):
+            q = peer_chip(k)
+            here = buf.at[slot(me)]
+            send(here, here, s_sem.at[q], r_sem.at[me], sib).wait_send()
+            there = buf.at[slot(q * CORES + core)]
+            send(there, there, f_sem.at[q], r_sem.at[me], sib).wait_send()
+            return carry
+
+        lax.fori_loop(1, chips, go, 0)
+        here = buf.at[slot(me)]
+        send(here, here, f_sem.at[chip], r_sem.at[me], sib).wait_send()
+
+    by_dev = lambda dev: dev
+    by_row = lambda dev: lax.rem(dev, CORES) * chips + dev // CORES
+
+    gather_start(gath, by_dev, g_send, g_fwd, g_recv)
+    c_copy = send(centers, csib, c_sem.at[0], c_sem.at[1], sib)
+    w_copy = send(wts, wsib, w_sem.at[0], w_sem.at[1], sib)
+    c_copy.start()
+    w_copy.start()
+    gather_start(gath2, by_dev, h_send, h_fwd, h_recv)
+
+    order = hot(pos_col == c_i.astype(F32))
+    c_sq = sq_col(centers[...])
+    c_sq_row = to_row(c_sq, held)
+    lab_row = labels[...].astype(F32)
+    lab_col = to_col(lab_row, rows_b)
+    first = core * half + chip * share
+    lab_here = jnp.sum(
+        jnp.where(iota((share, rows_b), 0) + first == iota((share, rows_b), 1), lab_row, 0.0),
+        axis=1, keepdims=True,
+    )
+
+    gather_pass(gath, by_dev, g_fwd, g_recv)
+    gather_rest(gath, by_dev, g_fwd, g_recv)
+    c_copy.wait_recv()
+    w_copy.wait_recv()
+
+    batch[...] = nn(order, gath[...].reshape(rows_b, width)).astype(BF16)
+    s_sq_row = to_row(sq_col(csib[...]), held)
+    rows = batch[pl.ds(pl.multiple_of(core * half, half), half), :]
+    rows_sq = sq_col(rows)
+    sums = nn(kern(rows, centers[...], rows_sq, c_sq_row), wts[...])
+    sums = sums + nn(kern(rows, csib[...], rows_sq, s_sq_row), wsib[...])
+    part[...] = sums.reshape(chips, share, cp)
+
+    def scatter(k, carry):
+        q = peer_chip(k)
+        send(part.at[q], recv.at[chip], r_send.at[q], r_recv.at[chip], q * CORES + core).start()
+        return carry
+
+    lax.fori_loop(1, chips, scatter, 0)
+
+    b_sq_row = to_row(sq_col(batch[...]), rows_b)
+    gather_pass(gath2, by_dev, h_fwd, h_recv)
+    kbz_t = kern(centers[...], batch[...], c_sq, b_sq_row).astype(F32)
+    gather_rest(gath2, by_dev, h_fwd, h_recv)
+    both = gath2[...].reshape(n * pair, width)
+    s_i, g_i = iota((subset, n * pair), 0), iota((subset, n * pair), 1)
+    spot = s_i + lax.div(s_i, sub_dev) * sub_dev
+    sub_rows = nn(hot(spot == g_i), both).astype(BF16)
+    vecs = nn(hot(spot + sub_dev == g_i), both).astype(BF16)[:, :rank]
+    sub_sq = sq_col(sub_rows)
+    kze = nn(kern(centers[...], sub_rows, c_sq, to_row(sub_sq, subset)), vecs)
+    proj = tn(vecs, kern(sub_rows, batch[...], sub_sq, b_sq_row))
+    to_grad = kbz_t - nn(kze * scales[...], proj, precision=HIGHEST)
+    to_sub = nn(eigvecs[...].astype(F32) * scales[...], proj, precision=HIGHEST)
+    high = to_grad.astype(BF16)
+    left[:held, :] = high
+    left[held:2 * held, :] = (to_grad - high.astype(F32)).astype(BF16)
+    sub_high = to_sub.astype(BF16).astype(F32)
+    left[2 * held:, :] = jnp.concatenate([sub_high, to_sub - sub_high], axis=0).astype(BF16)
+
+    total = part[chip]
+    for k in range(1, chips):
+        q = from_chip(k)
+        send(part.at[q], recv.at[q], r_send.at[q], r_recv.at[q], sib).wait_recv()
+        total = total + recv[q]
+    lanes = iota((share, cp), 1)
+    at_label = jnp.sum(
+        jnp.where(lanes.astype(F32) == lab_here, total - 1.0, 0.0), axis=1, keepdims=True
+    )
+    pred[by_row(me)] = jnp.where(lanes == classes, at_label, total).astype(BF16)
+
+    gather_start(pred, by_row, p_send, p_fwd, p_recv)
+    gather_pass(pred, by_row, p_fwd, p_recv)
+    gather_rest(pred, by_row, p_fwd, p_recv)
+
+    block = 128
+    for r in range(0, rows_b, block):
+        held_pred = pred[r // share:(r + block) // share].reshape(block, cp)
+        pred_out[r:r + block, :] = held_pred[:, :classes]
+        value = held_pred.astype(F32)
+        lanes = iota((block, cp), 1)
+        fix = jnp.sum(jnp.where(lanes == classes, value, 0.0), axis=1, keepdims=True)
+        resid[r:r + block, :] = jnp.where(
+            lanes.astype(F32) == lab_col[r:r + block], fix, value
+        ).astype(BF16)
+    out = nn(left[...], resid[...])
+    grad_out[...] = (out[:held] + out[held:2 * held]).astype(BF16)[:, :classes]
+    sub_out[...] = (out[2 * held:2 * held + sub_dev] + out[2 * held + sub_dev:])[:, :classes]
+
+    gather_end(gath, by_dev, g_send, g_fwd, g_recv)
+    gather_end(gath2, by_dev, h_send, h_fwd, h_recv)
+    gather_end(pred, by_row, p_send, p_fwd, p_recv)
+    c_copy.wait_send()
+    w_copy.wait_send()
+
+    def sent(k, carry):
+        q = peer_chip(k)
+        send(part.at[q], recv.at[chip], r_send.at[q], r_recv.at[chip], sib).wait_send()
+        return carry
+
+    lax.fori_loop(1, chips, sent, 0)
+
+
+def fused(n_blk, n_grid, centers, weights, batch_index, labels, sub_index, eigvecs, scales):
+    n = n_blk * n_grid
+    chips = n // CORES
+    held, width = centers.shape
+    classes = weights.shape[1]
+    rows_b = batch_index.shape[0]
+    sub_dev, rank = eigvecs.shape
+    share = rows_b // n
+    cp = pl.cdiv(classes + 1, 128) * 128
+    dma = pltpu.SemaphoreType.DMA
+    vmem = pl.BlockSpec(memory_space=pltpu.VMEM)
+    return pl.pallas_call(
+        functools.partial(body, n_grid, chips, share, classes),
+        out_shape=(
+            jax.ShapeDtypeStruct((rows_b, classes), BF16),
+            jax.ShapeDtypeStruct((held, classes), BF16),
+            jax.ShapeDtypeStruct((sub_dev, classes), F32),
+        ),
+        in_specs=[vmem] * 7,
+        out_specs=(vmem, vmem, vmem),
+        scratch_shapes=[
+            pltpu.VMEM((held, width), BF16),
+            pltpu.VMEM((held, cp), BF16),
+            pltpu.VMEM((held, cp), BF16),
+            pltpu.VMEM((n, share, width), BF16),
+            pltpu.VMEM((n, 2 * sub_dev, width), BF16),
+            pltpu.VMEM((rows_b, width), BF16),
+            pltpu.VMEM((chips, share, cp), F32),
+            pltpu.VMEM((chips, share, cp), F32),
+            pltpu.VMEM((n, share, cp), BF16),
+            pltpu.VMEM((2 * held + 2 * sub_dev, rows_b), BF16),
+            pltpu.VMEM((rows_b, cp), BF16),
+            dma((2,)), dma((2,)),
+            dma((chips,)), dma((chips,)), dma((n,)),
+            dma((chips,)), dma((chips,)), dma((n,)),
+            dma((chips,)), dma((chips,)), dma((n,)),
+            dma((chips,)), dma((chips,)),
+        ],
+        compiler_params=pltpu.CompilerParams(
+            collective_id=0, has_side_effects=True, vmem_limit_bytes=48 * 1024 * 1024
+        ),
+    )(
+        centers, weights, batch_index.reshape(1, rows_b), labels.reshape(1, rows_b),
+        sub_index.reshape(1, sub_dev), eigvecs, scales.reshape(1, rank),
+    )
+
+
 def solution(mesh):
+    n_blk, n_grid = mesh.shape["blk"], mesh.shape["grid"]
+    n = n_blk * n_grid
+
+    def step(centers, *rest):
+        rows_b, sub_dev = rest[1].shape[0], rest[4].shape[0]
+        whole_tiles = n_grid % CORES == 0 and rows_b % (16 * n) == 0 and sub_dev % 8 == 0
+        if whole_tiles:
+            return fused(n_blk, n_grid, centers, *rest)
+        return local(centers, *rest)
+
     return jax.shard_map(
-        local,
+        step,
         mesh=mesh,
         in_specs=(
             P(("blk", "grid"), None),

time: 215 us -> 63.6 us (0.30)
  the two profiles are of different devices: /device:TPU:1 before, /device:TPU:25 now
where the time goes in v1:
time: 63.6 us; the launch traced here: 63.4 us
  Pallas kernels  58.6 us (92%)
  local copies, waits for them, and re-layouts  4.11 us (6%)
  between operations  0.74 us (1%)
    pallas_call x1, Pallas kernels, fused(): pl.pallas_call(functools.partial(body, n_grid, chips, share, classes), ou...  58.6 us
    pallas_call x2, local copies, waits for them, and re-layouts, fused(): pl.pallas_call(functools.partial(body, n_grid, chips, share, classes), ou...  2.16 us
    unnamed x14, local copies, waits for them, and re-layouts  1.95 us

profile of v1, /device:TPU:25, one launch (start us, length us, event | category | flops | bytes accessed | tf_op | source)
XLA Modules:
  0.0 63.4 jit_solution(10933216644202807289)
XLA Ops:
  0.6 0.0 copy-start
  0.6 0.0 copy-start.1
  0.7 0.0 copy-start.2
  0.7 0.0 copy-start.3
  0.7 0.0 copy-start.4
  0.7 0.0 copy-start.5
  0.7 1.3 %copy.10.weights = f32[128,1000]{1,0:T(8,128)S(1)} copy(f32[128,1000]{0,1:T(8,128)} %param.8) | data formatting | bytes 1024000 | tf_op args[1]
  2.0 0.0 copy-done
  2.0 0.0 copy-done.1
  2.0 0.0 copy-done.2
  2.0 0.0 copy-done.3
  2.1 0.0 copy-done.4
  2.1 0.0 copy-done.5
  2.1 58.6 %shard_map.94 = (bf16[512,1000]{1,0:T(8,128)(2,1)S(1)}, bf16[128,1000]{1,0:T(8,128)(2,1)S(1)}, f32[8,1000]{1,0:T(8,128)S(1)}) custom-call(bf16[128,512]{1,0:T(8,128)(2,1)S(1)} %copy-done, f32[128,1000]{1,0:T(8,128)S(1)} %copy.10.weights, s32[1,512]{1,0:T(1,128)S(1)} %bitcast.4, s32[1,512]{1,0:T(1,128)S(1)} %bitcast.5, s32[1,8]{1,0:T(1,128)S(1)} %bitcast.7, ...), custom_call_target="tpu_custom_call" | custom-call | tf_op jit(solution)/shard_map/pallas_call | solution.py:348
  60.7 1.3 %copy.11 = bf16[512,1000]{0,1:T(8,128)(2,1)} copy(bf16[512,1000]{1,0:T(8,128)(2,1)S(1)} %get-tuple-element.3) | data formatting | bytes 2048000 | tf_op jit(solution)/shard_map/pallas_call | solution.py:348
  62.0 0.9 %copy.12 = bf16[128,1000]{0,1:T(8,128)(2,1)} copy(bf16[128,1000]{1,0:T(8,128)(2,1)S(1)} %get-tuple-element.4) | data formatting | bytes 512000 | tf_op jit(solution)/shard_map/pallas_call | solution.py:348
  62.8 0.6 copy.14
Async XLA Ops:
  0.6 1.4 %copy-start = (bf16[128,512]{1,0:T(8,128)(2,1)S(1)}, bf16[128,512]{1,0:T(8,128)(2,1)}, u32[]{:S(2)}) copy-start(bf16[128,512]{1,0:T(8,128)(2,1)} %centers.1) | copy-start | bytes 393220
  0.6 1.4 %copy-start.1 = (bf16[8,160]{1,0:T(8,128)(2,1)S(1)}, bf16[8,160]{1,0:T(8,128)(2,1)}, u32[]{:S(2)}) copy-start(bf16[8,160]{1,0:T(8,128)(2,1)} %eigvecs.1) | copy-start | bytes 7684
  0.7 1.4 %copy-start.2 = (s32[512]{0:T(512)S(1)}, s32[512]{0:T(512)}, u32[]{:S(2)}) copy-start(s32[512]{0:T(512)} %param.9) | copy-start | bytes 6148
  0.7 1.4 %copy-start.3 = (s32[512]{0:T(512)S(1)}, s32[512]{0:T(512)}, u32[]{:S(2)}) copy-start(s32[512]{0:T(512)} %param.10) | copy-start | bytes 6148
  0.7 1.4 %copy-start.4 = (f32[160]{0:T(256)S(1)}, f32[160]{0:T(256)}, u32[]{:S(2)}) copy-start(f32[160]{0:T(256)} %param.13) | copy-start | bytes 1924
  0.7 1.4 %copy-start.5 = (s32[8]{0:T(128)S(1)}, s32[8]{0:T(128)}, u32[]{:S(2)}) copy-start(s32[8]{0:T(128)} %param.11) | copy-start | bytes 100

commit v2 on v1

--- a/solution.py
+++ b/solution.py
@@ -104,25 +104,34 @@
 
 
 def body(
-    n_grid, chips, share, classes,
-    centers, weights, batch_index, labels, sub_index, eigvecs, scales,
+    n_blk, n_grid, share,
+    centers, weights_t, batch_index, labels, sub_index, eigvecs, scales,
     pred_out, grad_out, sub_out,
-    csib, wts, wsib, gath, gath2, batch, part, recv, pred, left, resid,
-    c_sem, w_sem, g_send, g_fwd, g_recv, h_send, h_fwd, h_recv,
-    p_send, p_fwd, p_recv, r_send, r_recv,
+    cbuf, wts, wbuf, gath, gath2, batch, part, recv, pred, fix, left, resid,
+    c_send, c_fwd, c_recv, w_send, w_fwd, w_recv, g_send, g_fwd, g_recv, h_send, h_fwd, h_recv,
+    pz_send, pp_send, ps_send, p_recv, r_send, r_recv,
 ):
     held, width = centers.shape
+    classes = weights_t.shape[0]
     rows_b = batch_index.shape[1]
-    cp = wts.shape[1]
+    gc, cs, _ = wts.shape
+    nz, rz, _ = part.shape
+    cp = gc * cs
     sub_dev, rank = eigvecs.shape
-    n = chips * CORES
+    n = n_blk * n_grid
+    chips = n // CORES
     subset = n * sub_dev
     half = rows_b // CORES
-    me = lax.axis_index("blk") * n_grid + lax.axis_index("grid")
+    blk, grid = lax.axis_index("blk"), lax.axis_index("grid")
+    me = blk * n_grid + grid
     chip, core = me // CORES, lax.rem(me, CORES)
+    z, j = grid // (2 * CORES), blk * 2 + lax.rem(grid // CORES, 2)
 
     def at(dev):
         return (dev // n_grid, lax.rem(dev, n_grid))
+
+    def dev_of(pj, pz, pc):
+        return (pj // 2) * n_grid + pz * 2 * CORES + lax.rem(pj, 2) * CORES + pc
 
     sib = chip * CORES + (1 - core)
 
@@ -142,9 +151,6 @@
 
     pl.semaphore_signal(barrier, inc=1, device_id=at(sib), device_id_type=MESH)
     lax.fori_loop(1, chips, greet, 0)
-
-    wts[...] = jnp.zeros_like(wts)
-    wts[:, :classes] = weights[...].astype(BF16)
 
     bi_row = batch_index[...].astype(F32)
     bi_col = to_col(bi_row, rows_b)
@@ -153,14 +159,20 @@
     r_i, c_i = iota((rows_b, rows_b), 0), iota((rows_b, rows_b), 1)
     same = own_col == own_row
     rank_row = jnp.sum(jnp.where(same, jnp.where(r_i < c_i, 1.0, 0.0), 0.0), axis=0, keepdims=True)
-    rank_col = jnp.sum(jnp.where(same, jnp.where(c_i < r_i, 1.0, 0.0), 0.0), axis=1, keepdims=True)
     pos_row = own_row * share + rank_row
-    pos_col = own_col * share + rank_col
     mine = (iota((share, rows_b), 0) + me * share).astype(F32)
     within = bi_col - own_col * held
     pick = hot(within == iota((rows_b, held), 1).astype(F32))
     sel = nn(hot(mine == pos_row), pick).astype(BF16)
     gath[me] = nn(sel, centers[...]).astype(BF16)
+
+    per = cs
+    for q in range(gc):
+        lo, hi = q * per, min((q + 1) * per, classes)
+        if hi - lo < cs:
+            wts[q] = jnp.zeros((cs, held), BF16)
+        if hi > lo:
+            wts[q, :hi - lo, :] = weights_t[lo:hi, :].astype(BF16)
 
     pair = 2 * sub_dev
     sub_col = jnp.sum(
@@ -187,94 +199,125 @@
             device_id=at(dev), device_id_type=MESH,
         )
 
-    def gather_start(buf, slot, s_sem, f_sem, r_sem):
+    def gather_start(buf, s_sem, f_sem, r_sem):
         def go(k, carry):
             q = peer_chip(k)
-            send(buf.at[slot(me)], buf.at[slot(me)], s_sem.at[q], r_sem.at[me],
-                 q * CORES + core).start()
+            send(buf.at[me], buf.at[me], s_sem.at[q], r_sem.at[me], q * CORES + core).start()
             return carry
 
         lax.fori_loop(1, chips, go, 0)
-        send(buf.at[slot(me)], buf.at[slot(me)], f_sem.at[chip], r_sem.at[me], sib).start()
-
-    def gather_pass(buf, slot, f_sem, r_sem):
+        send(buf.at[me], buf.at[me], f_sem.at[chip], r_sem.at[me], sib).start()
+
+    def gather_pass(buf, f_sem, r_sem):
         def go(k, carry):
             q = from_chip(k)
             dev = q * CORES + core
-            here = buf.at[slot(dev)]
-            send(here, here, f_sem.at[q], r_sem.at[dev], sib).wait_recv()
-            send(here, here, f_sem.at[q], r_sem.at[dev], sib).start()
+            send(buf.at[dev], buf.at[dev], f_sem.at[q], r_sem.at[dev], sib).wait_recv()
+            send(buf.at[dev], buf.at[dev], f_sem.at[q], r_sem.at[dev], sib).start()
             return carry
 
         lax.fori_loop(1, chips, go, 0)
 
-    def gather_rest(buf, slot, f_sem, r_sem):
+    def gather_rest(buf, f_sem, r_sem):
         def go(q, carry):
             dev = q * CORES + (1 - core)
-            here = buf.at[slot(dev)]
-            send(here, here, f_sem.at[q], r_sem.at[dev], sib).wait_recv()
+            send(buf.at[dev], buf.at[dev], f_sem.at[q], r_sem.at[dev], sib).wait_recv()
             return carry
 
         lax.fori_loop(0, chips, go, 0)
 
-    def gather_end(buf, slot, s_sem, f_sem, r_sem):
+    def gather_end(buf, s_sem, f_sem, r_sem):
         def go(k, carry):
             q = peer_chip(k)
-            here = buf.at[slot(me)]
-            send(here, here, s_sem.at[q], r_sem.at[me], sib).wait_send()
-            there = buf.at[slot(q * CORES + core)]
-            send(there, there, f_sem.at[q], r_sem.at[me], sib).wait_send()
+            send(buf.at[me], buf.at[me], s_sem.at[q], r_sem.at[me], sib).wait_send()
+            dev = q * CORES + core
+            send(buf.at[dev], buf.at[dev], f_sem.at[q], r_sem.at[me], sib).wait_send()
             return carry
 
         lax.fori_loop(1, chips, go, 0)
-        here = buf.at[slot(me)]
-        send(here, here, f_sem.at[chip], r_sem.at[me], sib).wait_send()
-
-    by_dev = lambda dev: dev
-    by_row = lambda dev: lax.rem(dev, CORES) * chips + dev // CORES
-
-    gather_start(gath, by_dev, g_send, g_fwd, g_recv)
-    c_copy = send(centers, csib, c_sem.at[0], c_sem.at[1], sib)
-    w_copy = send(wts, wsib, w_sem.at[0], w_sem.at[1], sib)
-    c_copy.start()
-    w_copy.start()
-    gather_start(gath2, by_dev, h_send, h_fwd, h_recv)
-
+        send(buf.at[me], buf.at[me], f_sem.at[chip], r_sem.at[me], sib).wait_send()
+
+    gather_start(gath, g_send, g_fwd, g_recv)
+
+    own = j * CORES + core
+    other = j * CORES + (1 - core)
+
+    def c_direct(q):
+        return send(centers, cbuf.at[own], c_send.at[q], c_recv.at[own], dev_of(q, z, core))
+
+    def w_direct(q):
+        return send(wts.at[q], wbuf.at[own], w_send.at[q], w_recv.at[own], dev_of(q, z, core))
+
+    def c_pass(q):
+        slot = q * CORES + core
+        return send(cbuf.at[slot], cbuf.at[slot], c_fwd.at[q], c_recv.at[slot], sib)
+
+    def w_pass(q):
+        slot = q * CORES + core
+        return send(wbuf.at[slot], wbuf.at[slot], w_fwd.at[q], w_recv.at[slot], sib)
+
+    c_own = send(centers, cbuf.at[own], c_send.at[j], c_recv.at[own], sib)
+    w_own = send(wts.at[j], wbuf.at[own], w_send.at[j], w_recv.at[own], sib)
+    c_own.start()
+    w_own.start()
+    near = [lax.rem(j + k, gc) for k in range(1, gc)]
+    for q in near:
+        c_direct(q).start()
+        w_direct(q).start()
+    gather_start(gath2, h_send, h_fwd, h_recv)
+
+    rank_col = jnp.sum(jnp.where(same, jnp.where(c_i < r_i, 1.0, 0.0), 0.0), axis=1, keepdims=True)
+    pos_col = own_col * share + rank_col
     order = hot(pos_col == c_i.astype(F32))
     c_sq = sq_col(centers[...])
     c_sq_row = to_row(c_sq, held)
     lab_row = labels[...].astype(F32)
     lab_col = to_col(lab_row, rows_b)
-    first = core * half + chip * share
+    first = core * half + z * rz
     lab_here = jnp.sum(
-        jnp.where(iota((share, rows_b), 0) + first == iota((share, rows_b), 1), lab_row, 0.0),
+        jnp.where(iota((rz, rows_b), 0) + first == iota((rz, rows_b), 1), lab_row, 0.0),
         axis=1, keepdims=True,
     )
 
-    gather_pass(gath, by_dev, g_fwd, g_recv)
-    gather_rest(gath, by_dev, g_fwd, g_recv)
-    c_copy.wait_recv()
-    w_copy.wait_recv()
+    gather_pass(gath, g_fwd, g_recv)
+    gather_rest(gath, g_fwd, g_recv)
 
     batch[...] = nn(order, gath[...].reshape(rows_b, width)).astype(BF16)
-    s_sq_row = to_row(sq_col(csib[...]), held)
     rows = batch[pl.ds(pl.multiple_of(core * half, half), half), :]
     rows_sq = sq_col(rows)
-    sums = nn(kern(rows, centers[...], rows_sq, c_sq_row), wts[...])
-    sums = sums + nn(kern(rows, csib[...], rows_sq, s_sq_row), wsib[...])
-    part[...] = sums.reshape(chips, share, cp)
-
-    def scatter(k, carry):
-        q = peer_chip(k)
-        send(part.at[q], recv.at[chip], r_send.at[q], r_recv.at[chip], q * CORES + core).start()
-        return carry
-
-    lax.fori_loop(1, chips, scatter, 0)
+
+    def add_from(slot):
+        there = cbuf[slot]
+        there_sq = to_row(sq_col(there), held)
+        return nt(kern(rows, there, rows_sq, there_sq), wbuf[slot])
+
+    part[...] = nt(kern(rows, centers[...], rows_sq, c_sq_row), wts[j]).reshape(nz, rz, cs)
+    send(cbuf.at[other], cbuf.at[other], c_fwd.at[j], c_recv.at[other], sib).wait_recv()
+    send(wbuf.at[other], wbuf.at[other], w_fwd.at[j], w_recv.at[other], sib).wait_recv()
+    part[...] += add_from(other).reshape(nz, rz, cs)
+    for q in near[::-1]:
+        c_pass(q).wait_recv()
+        c_pass(q).start()
+        w_pass(q).wait_recv()
+        w_pass(q).start()
+        part[...] += add_from(q * CORES + core).reshape(nz, rz, cs)
+    for q in near[::-1]:
+        slot = q * CORES + 1 - core
+        send(cbuf.at[slot], cbuf.at[slot], c_fwd.at[q], c_recv.at[slot], sib).wait_recv()
+        send(wbuf.at[slot], wbuf.at[slot], w_fwd.at[q], w_recv.at[slot], sib).wait_recv()
+        part[...] += add_from(slot).reshape(nz, rz, cs)
+
+    def sum_copy(q):
+        return send(part.at[q], recv.at[z], r_send.at[q], r_recv.at[z], dev_of(j, q, core))
+
+    along = [lax.rem(z + k, nz) for k in range(1, nz)]
+    for q in along:
+        sum_copy(q).start()
 
     b_sq_row = to_row(sq_col(batch[...]), rows_b)
-    gather_pass(gath2, by_dev, h_fwd, h_recv)
+    gather_pass(gath2, h_fwd, h_recv)
     kbz_t = kern(centers[...], batch[...], c_sq, b_sq_row).astype(F32)
-    gather_rest(gath2, by_dev, h_fwd, h_recv)
+    gather_rest(gath2, h_fwd, h_recv)
     both = gath2[...].reshape(n * pair, width)
     s_i, g_i = iota((subset, n * pair), 0), iota((subset, n * pair), 1)
     spot = s_i + lax.div(s_i, sub_dev) * sub_dev
@@ -291,47 +334,104 @@
     sub_high = to_sub.astype(BF16).astype(F32)
     left[2 * held:, :] = jnp.concatenate([sub_high, to_sub - sub_high], axis=0).astype(BF16)
 
-    total = part[chip]
-    for k in range(1, chips):
-        q = from_chip(k)
+    total = part[z]
+    for q in along[::-1]:
         send(part.at[q], recv.at[q], r_send.at[q], r_recv.at[q], sib).wait_recv()
         total = total + recv[q]
-    lanes = iota((share, cp), 1)
+    lanes = iota((rz, cs), 1) + j * cs
     at_label = jnp.sum(
         jnp.where(lanes.astype(F32) == lab_here, total - 1.0, 0.0), axis=1, keepdims=True
     )
-    pred[by_row(me)] = jnp.where(lanes == classes, at_label, total).astype(BF16)
-
-    gather_start(pred, by_row, p_send, p_fwd, p_recv)
-    gather_pass(pred, by_row, p_fwd, p_recv)
-    gather_rest(pred, by_row, p_fwd, p_recv)
-
-    block = 128
-    for r in range(0, rows_b, block):
-        held_pred = pred[r // share:(r + block) // share].reshape(block, cp)
-        pred_out[r:r + block, :] = held_pred[:, :classes]
+    spread = jnp.sum(
+        jnp.where(iota((rz, 128), 0) == iota((rz, 128), 1), at_label, 0.0), axis=0, keepdims=True
+    )
+    cols = pl.ds(pl.multiple_of(j * cs, 128), cs)
+    pred[core * nz + z, :, cols] = total.astype(BF16)
+    fix[me] = jnp.broadcast_to(spread, (16, 128)).astype(BF16)
+
+    def piece(t, pj, pz, pc):
+        if t == 0:
+            return pred.at[pc * nz + pz, :, pl.ds(pl.multiple_of(pj * cs, 128), cs)]
+        return fix.at[dev_of(pj, pz, pc)]
+
+    def pass_on(t, pj, pz, s_sem, dev):
+        here = piece(t, pj, pz, core)
+        return send(here, here, s_sem, p_recv.at[t, dev_of(pj, pz, core)], dev)
+
+    def to_z(t, q):
+        return pass_on(t, j, z, pz_send.at[t, q], dev_of(j, q, core))
+
+    def to_plane(t, pz, q):
+        return pass_on(t, j, pz, pp_send.at[t, pz * gc + q], dev_of(q, z, core))
+
+    def to_sib(t, pj, pz):
+        return pass_on(t, pj, pz, ps_send.at[t, pz * gc + pj], sib)
+
+    def arrived(t, pj, pz, pc):
+        here = piece(t, pj, pz, pc)
+        return send(here, here, ps_send.at[t, pz * gc + pj], p_recv.at[t, dev_of(pj, pz, pc)], sib)
+
+    for t in range(2):
+        for q in along:
+            to_z(t, q).start()
+    for t in range(2):
+        for q in near:
+            to_plane(t, z, q).start()
+        to_sib(t, j, z).start()
+    for pz in along[::-1]:
+        for t in range(2):
+            arrived(t, j, pz, core).wait_recv()
+            for q in near:
+                to_plane(t, pz, q).start()
+            to_sib(t, j, pz).start()
+    for pz in [z] + along[::-1]:
+        for q in near[::-1]:
+            for t in range(2):
+                arrived(t, q, pz, core).wait_recv()
+                to_sib(t, q, pz).start()
+    for pz in [z] + along[::-1]:
+        for q in [j] + near[::-1]:
+            for t in range(2):
+                arrived(t, q, pz, 1 - core).wait_recv()
+
+    for r in range(CORES * nz):
+        held_pred = pred[r]
+        lo = r * rz
+        pred_out[lo:lo + rz, :] = held_pred[:, :classes]
         value = held_pred.astype(F32)
-        lanes = iota((block, cp), 1)
-        fix = jnp.sum(jnp.where(lanes == classes, value, 0.0), axis=1, keepdims=True)
-        resid[r:r + block, :] = jnp.where(
-            lanes.astype(F32) == lab_col[r:r + block], fix, value
+        fixes = jnp.zeros((16, 128), F32)
+        for q in range(gc):
+            fixes = fixes + fix[dev_of(q, r % nz, r // nz)].astype(F32)
+        fix_col = jnp.sum(
+            jnp.where(iota((rz, 128), 0) == iota((rz, 128), 1), fixes[:1], 0.0),
+            axis=1, keepdims=True,
+        )
+        resid[lo:lo + rz, :] = jnp.where(
+            iota((rz, cp), 1).astype(F32) == lab_col[lo:lo + rz], fix_col, value
         ).astype(BF16)
     out = nn(left[...], resid[...])
     grad_out[...] = (out[:held] + out[held:2 * held]).astype(BF16)[:, :classes]
     sub_out[...] = (out[2 * held:2 * held + sub_dev] + out[2 * held + sub_dev:])[:, :classes]
 
-    gather_end(gath, by_dev, g_send, g_fwd, g_recv)
-    gather_end(gath2, by_dev, h_send, h_fwd, h_recv)
-    gather_end(pred, by_row, p_send, p_fwd, p_recv)
-    c_copy.wait_send()
-    w_copy.wait_send()
-
-    def sent(k, carry):
-        q = peer_chip(k)
-        send(part.at[q], recv.at[chip], r_send.at[q], r_recv.at[chip], sib).wait_send()
-        return carry
-
-    lax.fori_loop(1, chips, sent, 0)
+    gather_end(gath, g_send, g_fwd, g_recv)
+    gather_end(gath2, h_send, h_fwd, h_recv)
+    c_own.wait_send()
+    w_own.wait_send()
+    for q in near:
+        c_direct(q).wait_send()
+        w_direct(q).wait_send()
+        c_pass(q).wait_send()
+        w_pass(q).wait_send()
+    for q in along:
+        sum_copy(q).wait_send()
+    for t in range(2):
+        for q in along:
+            to_z(t, q).wait_send()
+        for pz in [z] + along:
+            for q in near:
+                to_plane(t, pz, q).wait_send()
+            for q in [j] + near:
+                to_sib(t, q, pz).wait_send()
 
 
 def fused(n_blk, n_grid, centers, weights, batch_index, labels, sub_index, eigvecs, scales):
@@ -342,11 +442,13 @@
     rows_b = batch_index.shape[0]
     sub_dev, rank = eigvecs.shape
     share = rows_b // n
-    cp = pl.cdiv(classes + 1, 128) * 128
+    gc, nz = n_blk * 2, n_grid // (2 * CORES)
+    cs = pl.cdiv(classes, gc * 128) * 128
+    rz = rows_b // (CORES * nz)
     dma = pltpu.SemaphoreType.DMA
     vmem = pl.BlockSpec(memory_space=pltpu.VMEM)
     return pl.pallas_call(
-        functools.partial(body, n_grid, chips, share, classes),
+        functools.partial(body, n_blk, n_grid, share),
         out_shape=(
             jax.ShapeDtypeStruct((rows_b, classes), BF16),
             jax.ShapeDtypeStruct((held, classes), BF16),
@@ -355,28 +457,30 @@
         in_specs=[vmem] * 7,
         out_specs=(vmem, vmem, vmem),
         scratch_shapes=[
-            pltpu.VMEM((held, width), BF16),
-            pltpu.VMEM((held, cp), BF16),
-            pltpu.VMEM((held, cp), BF16),
+            pltpu.VMEM((gc * CORES, held, width), BF16),
+            pltpu.VMEM((gc, cs, held), BF16),
+            pltpu.VMEM((gc * CORES, cs, held), BF16),
             pltpu.VMEM((n, share, width), BF16),
             pltpu.VMEM((n, 2 * sub_dev, width), BF16),
             pltpu.VMEM((rows_b, width), BF16),
-            pltpu.VMEM((chips, share, cp), F32),
-            pltpu.VMEM((chips, share, cp), F32),
-            pltpu.VMEM((n, share, cp), BF16),
+            pltpu.VMEM((nz, rz, cs), F32),
+            pltpu.VMEM((nz, rz, cs), F32),
+            pltpu.VMEM((CORES * nz, rz, gc * cs), BF16),
+            pltpu.VMEM((n, 16, 128), BF16),
             pltpu.VMEM((2 * held + 2 * sub_dev, rows_b), BF16),
-            pltpu.VMEM((rows_b, cp), BF16),
-            dma((2,)), dma((2,)),
+            pltpu.VMEM((rows_b, gc * cs), BF16),
+            dma((gc,)), dma((gc,)), dma((gc * CORES,)),
+            dma((gc,)), dma((gc,)), dma((gc * CORES,)),
             dma((chips,)), dma((chips,)), dma((n,)),
             dma((chips,)), dma((chips,)), dma((n,)),
-            dma((chips,)), dma((chips,)), dma((n,)),
-            dma((chips,)), dma((chips,)),
+            dma((2, nz)), dma((2, nz * gc)), dma((2, nz * gc)), dma((2, n)),
+            dma((nz,)), dma((nz,)),
         ],
         compiler_params=pltpu.CompilerParams(
             collective_id=0, has_side_effects=True, vmem_limit_bytes=48 * 1024 * 1024
         ),
     )(
-        centers, weights, batch_index.reshape(1, rows_b), labels.reshape(1, rows_b),
+        centers, weights.T, batch_index.reshape(1, rows_b), labels.reshape(1, rows_b),
         sub_index.reshape(1, sub_dev), eigvecs, scales.reshape(1, rank),
     )
 
@@ -387,7 +491,11 @@
 
     def step(centers, *rest):
         rows_b, sub_dev = rest[1].shape[0], rest[4].shape[0]
-        whole_tiles = n_grid % CORES == 0 and rows_b % (16 * n) == 0 and sub_dev % 8 == 0
+        nz = n_grid // (2 * CORES)
+        whole_tiles = (
+            n_grid % (2 * CORES) == 0 and rows_b % (16 * n) == 0 and sub_dev % 8 == 0
+            and rows_b <= 128 * CORES * nz
+        )
         if whole_tiles:
             return fused(n_blk, n_grid, centers, *rest)
         return local(centers, *rest)

time: 63.6 us -> 53.6 us (0.84)
  the two profiles are of different devices: /device:TPU:25 before, /device:TPU:1 now
where the time goes in v2:
time: 53.6 us; the launch traced here: 53.4 us
  Pallas kernels  46.7 us (87%)
  local copies, waits for them, and re-layouts  6.06 us (11%)
  between operations  0.68 us (1%)
    pallas_call x1, Pallas kernels, fused(): pl.pallas_call(functools.partial(body, n_blk, n_grid, share), out_shape=(...  46.7 us
    unnamed x15, local copies, waits for them, and re-layouts  3.9 us
    pallas_call x2, local copies, waits for them, and re-layouts, fused(): pl.pallas_call(functools.partial(body, n_blk, n_grid, share), out_shape=(...  2.16 us

profile of v2, /device:TPU:1, one launch (start us, length us, event | category | flops | bytes accessed | tf_op | source)
XLA Modules:
  0.0 53.4 jit_solution(3080906828057152914)
XLA Ops:
  0.6 0.0 copy-start.4
  0.6 0.0 copy-start.2
  0.7 0.0 copy-start.3
  0.7 0.0 copy-start.5
  0.7 0.6 %copy-done.4 = s32[512]{0:T(512)S(1)} copy-done((s32[512]{0:T(512)S(1)}, s32[512]{0:T(512)}, u32[]{:S(2)}) %copy-start.4) | copy-done | bytes 2072
  1.3 0.0 copy-done.2
  1.3 0.0 copy-done.3
  1.3 0.0 copy-done.5
  1.4 0.0 copy-start
  1.4 1.0 %copy-done = f32[128,1000]{0,1:T(8,128)S(1)} copy-done((f32[128,1000]{0,1:T(8,128)S(1)}, f32[128,1000]{0,1:T(8,128)}, u32[]{:S(2)}) %copy-start) | copy-done | bytes 512024
  2.4 0.0 copy-start.1
  2.4 0.9 %copy-done.1 = bf16[128,512]{1,0:T(8,128)(2,1)S(1)} copy-done((bf16[128,512]{1,0:T(8,128)(2,1)S(1)}, bf16[128,512]{1,0:T(8,128)(2,1)}, u32[]{:S(2)}) %copy-start.1) | copy-done | bytes 131096
  3.3 0.0 copy-start.6
  3.3 0.7 %copy-done.6 = s32[8]{0:T(128)S(1)} copy-done((s32[8]{0:T(128)S(1)}, s32[8]{0:T(128)}, u32[]{:S(2)}) %copy-start.6) | copy-done | bytes 56
  4.0 46.7 %shard_map.94 = (bf16[512,1000]{1,0:T(8,128)(2,1)S(1)}, bf16[128,1000]{1,0:T(8,128)(2,1)S(1)}, f32[8,1000]{1,0:T(8,128)S(1)}) custom-call(bf16[128,512]{1,0:T(8,128)(2,1)S(1)} %copy-done.1, f32[1000,128]{1,0:T(8,128)S(1)} %bitcast.5, s32[1,512]{1,0:T(1,128)S(1)} %bitcast.6, s32[1,512]{1,0:T(1,128)S(1)} %bitcast.7, s32[1,8]{1,0:T(1,128)S(1)} %bitcast.9, ...), custom_call_target="tpu_custom_call" | custom-call | tf_op jit(solution)/shard_map/pallas_call | solution.py:450
  50.6 1.3 %copy.10 = bf16[512,1000]{0,1:T(8,128)(2,1)} copy(bf16[512,1000]{1,0:T(8,128)(2,1)S(1)} %get-tuple-element.3) | data formatting | bytes 2048000 | tf_op jit(solution)/shard_map/pallas_call | solution.py:450
  51.9 0.9 %copy.11 = bf16[128,1000]{0,1:T(8,128)(2,1)} copy(bf16[128,1000]{1,0:T(8,128)(2,1)S(1)} %get-tuple-element.4) | data formatting | bytes 512000 | tf_op jit(solution)/shard_map/pallas_call | solution.py:450
  52.8 0.6 %copy.13 = f32[8,1000]{1,0:T(8,128)} copy(f32[8,1000]{1,0:T(8,128)S(1)} %get-tuple-element.11) | data formatting | bytes 64000
Async XLA Ops:
  0.6 0.7 %copy-start.4 = (s32[512]{0:T(512)S(1)}, s32[512]{0:T(512)}, u32[]{:S(2)}) copy-start(s32[512]{0:T(512)} %param.10) | copy-start | bytes 6148
  0.6 0.7 %copy-start.2 = (bf16[8,160]{1,0:T(8,128)(2,1)S(1)}, bf16[8,160]{1,0:T(8,128)(2,1)}, u32[]{:S(2)}) copy-start(bf16[8,160]{1,0:T(8,128)(2,1)} %eigvecs.1) | copy-start | bytes 7684
  0.7 0.7 %copy-start.3 = (s32[512]{0:T(512)S(1)}, s32[512]{0:T(512)}, u32[]{:S(2)}) copy-start(s32[512]{0:T(512)} %param.9) | copy-start | bytes 6148
  0.7 0.7 %copy-start.5 = (f32[160]{0:T(256)S(1)}, f32[160]{0:T(256)}, u32[]{:S(2)}) copy-start(f32[160]{0:T(256)} %param.13) | copy-start | bytes 1924
  1.4 1.0 %copy-start = (f32[128,1000]{0,1:T(8,128)S(1)}, f32[128,1000]{0,1:T(8,128)}, u32[]{:S(2)}) copy-start(f32[128,1000]{0,1:T(8,128)} %param.8) | copy-start | bytes 1536004
  2.4 0.9 %copy-start.1 = (bf16[128,512]{1,0:T(8,128)(2,1)S(1)}, bf16[128,512]{1,0:T(8,128)(2,1)}, u32[]{:S(2)}) copy-start(bf16[128,512]{1,0:T(8,128)(2,1)} %centers.1) | copy-start | bytes 393220
  3.3 0.7 %copy-start.6 = (s32[8]{0:T(128)S(1)}, s32[8]{0:T(128)}, u32[]{:S(2)}) copy-start(s32[8]{0:T(128)} %param.11) | copy-start | bytes 100

commit v3 on v2

--- a/solution.py
+++ b/solution.py
@@ -107,7 +107,7 @@
     n_blk, n_grid, share,
     centers, weights_t, batch_index, labels, sub_index, eigvecs, scales,
     pred_out, grad_out, sub_out,
-    cbuf, wts, wbuf, gath, gath2, batch, part, recv, pred, fix, left, resid,
+    cbuf, wts, wbuf, gath, gath2, batch, part, recv, pred, fix, left, resid, lab_buf,
     c_send, c_fwd, c_recv, w_send, w_fwd, w_recv, g_send, g_fwd, g_recv, h_send, h_fwd, h_recv,
     pz_send, pp_send, ps_send, p_recv, r_send, r_recv,
 ):
@@ -153,17 +153,14 @@
     lax.fori_loop(1, chips, greet, 0)
 
     bi_row = batch_index[...].astype(F32)
-    bi_col = to_col(bi_row, rows_b)
     own_row = jnp.floor((bi_row + 0.5) * (1.0 / held))
-    own_col = jnp.floor((bi_col + 0.5) * (1.0 / held))
     r_i, c_i = iota((rows_b, rows_b), 0), iota((rows_b, rows_b), 1)
-    same = own_col == own_row
-    rank_row = jnp.sum(jnp.where(same, jnp.where(r_i < c_i, 1.0, 0.0), 0.0), axis=0, keepdims=True)
-    pos_row = own_row * share + rank_row
-    mine = (iota((share, rows_b), 0) + me * share).astype(F32)
-    within = bi_col - own_col * held
-    pick = hot(within == iota((rows_b, held), 1).astype(F32))
-    sel = nn(hot(mine == pos_row), pick).astype(BF16)
+    here_row = jnp.broadcast_to(jnp.where(own_row == me.astype(F32), 1.0, 0.0), (16, rows_b))
+    ahead = nn(here_row.astype(BF16), hot(r_i < c_i))[:1]
+    nth = jnp.where(own_row == me.astype(F32), ahead, -1.0)
+    within = bi_row - own_row * held
+    pick = hot(iota((held, rows_b), 0).astype(F32) == within)
+    sel = nt(hot(iota((share, rows_b), 0).astype(F32) == nth), pick).astype(BF16)
     gath[me] = nn(sel, centers[...]).astype(BF16)
 
     per = cs
@@ -173,23 +170,6 @@
             wts[q] = jnp.zeros((cs, held), BF16)
         if hi > lo:
             wts[q, :hi - lo, :] = weights_t[lo:hi, :].astype(BF16)
-
-    pair = 2 * sub_dev
-    sub_col = jnp.sum(
-        jnp.where(
-            iota((pair, sub_dev), 0) == iota((pair, sub_dev), 1),
-            sub_index[...].astype(F32), 0.0,
-        ),
-        axis=1, keepdims=True,
-    )
-    sub_hot = hot(
-        (iota((pair, held), 0) < sub_dev) & (sub_col == iota((pair, held), 1).astype(F32))
-    )
-    eig16 = nn(
-        hot(iota((pair, sub_dev), 0) == iota((pair, sub_dev), 1) + sub_dev), eigvecs[...]
-    ).astype(BF16)
-    eig16 = nn(eig16, hot(iota((rank, width), 0) == iota((rank, width), 1)))
-    gath2[me] = (nn(sub_hot, centers[...]) + eig16).astype(BF16)
 
     pl.semaphore_wait(barrier, chips)
 
@@ -264,15 +244,35 @@
     for q in near:
         c_direct(q).start()
         w_direct(q).start()
+    pair = 2 * sub_dev
+    sub_col = jnp.sum(
+        jnp.where(
+            iota((pair, sub_dev), 0) == iota((pair, sub_dev), 1),
+            sub_index[...].astype(F32), 0.0,
+        ),
+        axis=1, keepdims=True,
+    )
+    sub_hot = hot(
+        (iota((pair, held), 0) < sub_dev) & (sub_col == iota((pair, held), 1).astype(F32))
+    )
+    eig16 = nn(
+        hot(iota((pair, sub_dev), 0) == iota((pair, sub_dev), 1) + sub_dev), eigvecs[...]
+    ).astype(BF16)
+    eig16 = nn(eig16, hot(iota((rank, width), 0) == iota((rank, width), 1)))
+    gath2[me] = (nn(sub_hot, centers[...]) + eig16).astype(BF16)
+
     gather_start(gath2, h_send, h_fwd, h_recv)
 
+    bi_col = to_col(bi_row, rows_b)
+    own_col = jnp.floor((bi_col + 0.5) * (1.0 / held))
+    same = own_col == own_row
     rank_col = jnp.sum(jnp.where(same, jnp.where(c_i < r_i, 1.0, 0.0), 0.0), axis=1, keepdims=True)
     pos_col = own_col * share + rank_col
     order = hot(pos_col == c_i.astype(F32))
     c_sq = sq_col(centers[...])
     c_sq_row = to_row(c_sq, held)
     lab_row = labels[...].astype(F32)
-    lab_col = to_col(lab_row, rows_b)
+    lab_buf[...] = jnp.broadcast_to(to_col(lab_row, rows_b), (rows_b, 128))
     first = core * half + z * rz
     lab_here = jnp.sum(
         jnp.where(iota((rz, rows_b), 0) + first == iota((rz, rows_b), 1), lab_row, 0.0),
@@ -384,32 +384,39 @@
             for q in near:
                 to_plane(t, pz, q).start()
             to_sib(t, j, pz).start()
+    def finish(pz, pc):
+        lo = pl.multiple_of((pc * nz + pz) * rz, rz)
+        held_pred = pred[pc * nz + pz]
+        pred_out[pl.ds(lo, rz), :] = held_pred[:, :classes]
+        fixes = jnp.zeros((16, 128), F32)
+        for q in range(gc):
+            fixes = fixes + fix[dev_of(q, pz, pc)].astype(F32)
+        fix_col = jnp.sum(
+            jnp.where(iota((rz, 128), 0) == iota((rz, 128), 1), fixes[:1], 0.0),
+            axis=1, keepdims=True,
+        )
+        resid[pl.ds(lo, rz), :] = jnp.where(
+            iota((rz, cp), 1).astype(F32) == lab_buf[pl.ds(lo, rz), :][:, :1],
+            fix_col, held_pred.astype(F32),
+        ).astype(BF16)
+
+    def apply(pc):
+        span = pl.ds(pl.multiple_of(pc * half, half), half)
+        return nn(left[:, span], resid[span, :])
+
     for pz in [z] + along[::-1]:
         for q in near[::-1]:
             for t in range(2):
                 arrived(t, q, pz, core).wait_recv()
                 to_sib(t, q, pz).start()
+        finish(pz, core)
+    out = apply(core)
     for pz in [z] + along[::-1]:
         for q in [j] + near[::-1]:
             for t in range(2):
                 arrived(t, q, pz, 1 - core).wait_recv()
-
-    for r in range(CORES * nz):
-        held_pred = pred[r]
-        lo = r * rz
-        pred_out[lo:lo + rz, :] = held_pred[:, :classes]
-        value = held_pred.astype(F32)
-        fixes = jnp.zeros((16, 128), F32)
-        for q in range(gc):
-            fixes = fixes + fix[dev_of(q, r % nz, r // nz)].astype(F32)
-        fix_col = jnp.sum(
-            jnp.where(iota((rz, 128), 0) == iota((rz, 128), 1), fixes[:1], 0.0),
-            axis=1, keepdims=True,
-        )
-        resid[lo:lo + rz, :] = jnp.where(
-            iota((rz, cp), 1).astype(F32) == lab_col[lo:lo + rz], fix_col, value
-        ).astype(BF16)
-    out = nn(left[...], resid[...])
+        finish(pz, 1 - core)
+    out = out + apply(1 - core)
     grad_out[...] = (out[:held] + out[held:2 * held]).astype(BF16)[:, :classes]
     sub_out[...] = (out[2 * held:2 * held + sub_dev] + out[2 * held + sub_dev:])[:, :classes]
 
@@ -469,6 +476,7 @@
             pltpu.VMEM((n, 16, 128), BF16),
             pltpu.VMEM((2 * held + 2 * sub_dev, rows_b), BF16),
             pltpu.VMEM((rows_b, gc * cs), BF16),
+            pltpu.VMEM((rows_b, 128), F32),
             dma((gc,)), dma((gc,)), dma((gc * CORES,)),
             dma((gc,)), dma((gc,)), dma((gc * CORES,)),
             dma((chips,)), dma((chips,)), dma((n,)),
@@ -494,7 +502,7 @@
         nz = n_grid // (2 * CORES)
         whole_tiles = (
             n_grid % (2 * CORES) == 0 and rows_b % (16 * n) == 0 and sub_dev % 8 == 0
-            and rows_b <= 128 * CORES * nz
+            and rows_b <= 128 * CORES * nz and rows_b % (128 * CORES) == 0
         )
         if whole_tiles:
             return fused(n_blk, n_grid, centers, *rest)

time: 53.6 us -> 53.6 us (level)
  no operation moved by 1% of the time
where the time goes in v3:
time: 53.6 us; the launch traced here: 53.4 us
  Pallas kernels  46.6 us (87%)
  local copies, waits for them, and re-layouts  6.06 us (11%)
  between operations  0.68 us (1%)
    pallas_call x1, Pallas kernels, fused(): pl.pallas_call(functools.partial(body, n_blk, n_grid, share), out_shape=(...  46.6 us
    unnamed x15, local copies, waits for them, and re-layouts  3.9 us
    pallas_call x2, local copies, waits for them, and re-layouts, fused(): pl.pallas_call(functools.partial(body, n_blk, n_grid, share), out_shape=(...  2.16 us

profile of v3, /device:TPU:1, one launch (start us, length us, event | category | flops | bytes accessed | tf_op | source)
XLA Modules:
  0.0 53.4 jit_solution(13354402968594517461)
XLA Ops:
  0.6 0.0 copy-start.4
  0.6 0.0 copy-start.2
  0.7 0.0 copy-start.3
  0.7 0.0 copy-start.5
  0.7 0.6 %copy-done.4 = s32[512]{0:T(512)S(1)} copy-done((s32[512]{0:T(512)S(1)}, s32[512]{0:T(512)}, u32[]{:S(2)}) %copy-start.4) | copy-done | bytes 2072
  1.3 0.0 copy-done.2
  1.3 0.0 copy-done.3
  1.3 0.0 copy-done.5
  1.4 0.0 copy-start
  1.4 1.0 %copy-done = f32[128,1000]{0,1:T(8,128)S(1)} copy-done((f32[128,1000]{0,1:T(8,128)S(1)}, f32[128,1000]{0,1:T(8,128)}, u32[]{:S(2)}) %copy-start) | copy-done | bytes 512024
  2.4 0.0 copy-start.1
  2.4 0.9 %copy-done.1 = bf16[128,512]{1,0:T(8,128)(2,1)S(1)} copy-done((bf16[128,512]{1,0:T(8,128)(2,1)S(1)}, bf16[128,512]{1,0:T(8,128)(2,1)}, u32[]{:S(2)}) %copy-start.1) | copy-done | bytes 131096
  3.3 0.0 copy-start.6
  3.3 0.7 %copy-done.6 = s32[8]{0:T(128)S(1)} copy-done((s32[8]{0:T(128)S(1)}, s32[8]{0:T(128)}, u32[]{:S(2)}) %copy-start.6) | copy-done | bytes 56
  4.0 46.6 %shard_map.94 = (bf16[512,1000]{1,0:T(8,128)(2,1)S(1)}, bf16[128,1000]{1,0:T(8,128)(2,1)S(1)}, f32[8,1000]{1,0:T(8,128)S(1)}) custom-call(bf16[128,512]{1,0:T(8,128)(2,1)S(1)} %copy-done.1, f32[1000,128]{1,0:T(8,128)S(1)} %bitcast.5, s32[1,512]{1,0:T(1,128)S(1)} %bitcast.6, s32[1,512]{1,0:T(1,128)S(1)} %bitcast.7, s32[1,8]{1,0:T(1,128)S(1)} %bitcast.9, ...), custom_call_target="tpu_custom_call" | custom-call | tf_op jit(solution)/shard_map/pallas_call | solution.py:457
  50.6 1.3 %copy.10 = bf16[512,1000]{0,1:T(8,128)(2,1)} copy(bf16[512,1000]{1,0:T(8,128)(2,1)S(1)} %get-tuple-element.3) | data formatting | bytes 2048000 | tf_op jit(solution)/shard_map/pallas_call | solution.py:457
  51.9 0.9 %copy.11 = bf16[128,1000]{0,1:T(8,128)(2,1)} copy(bf16[128,1000]{1,0:T(8,128)(2,1)S(1)} %get-tuple-element.4) | data formatting | bytes 512000 | tf_op jit(solution)/shard_map/pallas_call | solution.py:457
  52.8 0.6 %copy.13 = f32[8,1000]{1,0:T(8,128)} copy(f32[8,1000]{1,0:T(8,128)S(1)} %get-tuple-element.11) | data formatting | bytes 64000
Async XLA Ops:
  0.6 0.7 %copy-start.4 = (s32[512]{0:T(512)S(1)}, s32[512]{0:T(512)}, u32[]{:S(2)}) copy-start(s32[512]{0:T(512)} %param.10) | copy-start | bytes 6148
  0.6 0.7 %copy-start.2 = (bf16[8,160]{1,0:T(8,128)(2,1)S(1)}, bf16[8,160]{1,0:T(8,128)(2,1)}, u32[]{:S(2)}) copy-start(bf16[8,160]{1,0:T(8,128)(2,1)} %eigvecs.1) | copy-start | bytes 7684
  0.7 0.7 %copy-start.3 = (s32[512]{0:T(512)S(1)}, s32[512]{0:T(512)}, u32[]{:S(2)}) copy-start(s32[512]{0:T(512)} %param.9) | copy-start | bytes 6148
  0.7 0.7 %copy-start.5 = (f32[160]{0:T(256)S(1)}, f32[160]{0:T(256)}, u32[]{:S(2)}) copy-start(f32[160]{0:T(256)} %param.13) | copy-start | bytes 1924
  1.4 1.0 %copy-start = (f32[128,1000]{0,1:T(8,128)S(1)}, f32[128,1000]{0,1:T(8,128)}, u32[]{:S(2)}) copy-start(f32[128,1000]{0,1:T(8,128)} %param.8) | copy-start | bytes 1536004
  2.4 0.9 %copy-start.1 = (bf16[128,512]{1,0:T(8,128)(2,1)S(1)}, bf16[128,512]{1,0:T(8,128)(2,1)}, u32[]{:S(2)}) copy-start(bf16[128,512]{1,0:T(8,128)(2,1)} %centers.1) | copy-start | bytes 393220
  3.3 0.7 %copy-start.6 = (s32[8]{0:T(128)S(1)}, s32[8]{0:T(128)}, u32[]{:S(2)}) copy-start(s32[8]{0:T(128)} %param.11) | copy-start | bytes 100

commit v4 on v3

--- a/solution.py
+++ b/solution.py
@@ -100,7 +100,7 @@
 
 def kern(left, right, left_sq, right_sq):
     dist = jnp.sqrt(jnp.maximum(left_sq + right_sq - 2.0 * nt(left, right), 0.0) + SOFTEN)
-    return jnp.exp(-dist / SPREAD).astype(BF16)
+    return jnp.exp(dist * (-1.0 / SPREAD)).astype(BF16)
 
 
 def body(
@@ -317,6 +317,55 @@
     b_sq_row = to_row(sq_col(batch[...]), rows_b)
     gather_pass(gath2, h_fwd, h_recv)
     kbz_t = kern(centers[...], batch[...], c_sq, b_sq_row).astype(F32)
+    total = part[z]
+    for q in along[::-1]:
+        send(part.at[q], recv.at[q], r_send.at[q], r_recv.at[q], sib).wait_recv()
+        total = total + recv[q]
+    lanes = iota((rz, cs), 1) + j * cs
+    at_label = jnp.sum(
+        jnp.where(lanes.astype(F32) == lab_here, total - 1.0, 0.0), axis=1, keepdims=True
+    )
+    spread = jnp.sum(
+        jnp.where(iota((rz, 128), 0) == iota((rz, 128), 1), at_label, 0.0), axis=0, keepdims=True
+    )
+    pred[me] = total.astype(BF16)
+    fix[me] = jnp.broadcast_to(spread, (16, 128)).astype(BF16)
+
+    def piece(t, pj, pz, pc):
+        if t == 0:
+            return pred.at[dev_of(pj, pz, pc)]
+        return fix.at[dev_of(pj, pz, pc)]
+
+    def pass_on(t, pj, pz, s_sem, dev):
+        here = piece(t, pj, pz, core)
+        return send(here, here, s_sem, p_recv.at[t, dev_of(pj, pz, core)], dev)
+
+    def to_z(t, q):
+        return pass_on(t, j, z, pz_send.at[t, q], dev_of(j, q, core))
+
+    def to_plane(t, pz, q):
+        return pass_on(t, j, pz, pp_send.at[t, pz * gc + q], dev_of(q, z, core))
+
+    def to_sib(t, pj, pz):
+        return pass_on(t, pj, pz, ps_send.at[t, pz * gc + pj], sib)
+
+    def arrived(t, pj, pz, pc):
+        here = piece(t, pj, pz, pc)
+        return send(here, here, ps_send.at[t, pz * gc + pj], p_recv.at[t, dev_of(pj, pz, pc)], sib)
+
+    for t in range(2):
+        for q in along:
+            to_z(t, q).start()
+    for t in range(2):
+        for q in near:
+            to_plane(t, z, q).start()
+        to_sib(t, j, z).start()
+    for pz in along[::-1]:
+        for t in range(2):
+            arrived(t, j, pz, core).wait_recv()
+            for q in near:
+                to_plane(t, pz, q).start()
+            to_sib(t, j, pz).start()
     gather_rest(gath2, h_fwd, h_recv)
     both = gath2[...].reshape(n * pair, width)
     s_i, g_i = iota((subset, n * pair), 0), iota((subset, n * pair), 1)
@@ -334,59 +383,9 @@
     sub_high = to_sub.astype(BF16).astype(F32)
     left[2 * held:, :] = jnp.concatenate([sub_high, to_sub - sub_high], axis=0).astype(BF16)
 
-    total = part[z]
-    for q in along[::-1]:
-        send(part.at[q], recv.at[q], r_send.at[q], r_recv.at[q], sib).wait_recv()
-        total = total + recv[q]
-    lanes = iota((rz, cs), 1) + j * cs
-    at_label = jnp.sum(
-        jnp.where(lanes.astype(F32) == lab_here, total - 1.0, 0.0), axis=1, keepdims=True
-    )
-    spread = jnp.sum(
-        jnp.where(iota((rz, 128), 0) == iota((rz, 128), 1), at_label, 0.0), axis=0, keepdims=True
-    )
-    cols = pl.ds(pl.multiple_of(j * cs, 128), cs)
-    pred[core * nz + z, :, cols] = total.astype(BF16)
-    fix[me] = jnp.broadcast_to(spread, (16, 128)).astype(BF16)
-
-    def piece(t, pj, pz, pc):
-        if t == 0:
-            return pred.at[pc * nz + pz, :, pl.ds(pl.multiple_of(pj * cs, 128), cs)]
-        return fix.at[dev_of(pj, pz, pc)]
-
-    def pass_on(t, pj, pz, s_sem, dev):
-        here = piece(t, pj, pz, core)
-        return send(here, here, s_sem, p_recv.at[t, dev_of(pj, pz, core)], dev)
-
-    def to_z(t, q):
-        return pass_on(t, j, z, pz_send.at[t, q], dev_of(j, q, core))
-
-    def to_plane(t, pz, q):
-        return pass_on(t, j, pz, pp_send.at[t, pz * gc + q], dev_of(q, z, core))
-
-    def to_sib(t, pj, pz):
-        return pass_on(t, pj, pz, ps_send.at[t, pz * gc + pj], sib)
-
-    def arrived(t, pj, pz, pc):
-        here = piece(t, pj, pz, pc)
-        return send(here, here, ps_send.at[t, pz * gc + pj], p_recv.at[t, dev_of(pj, pz, pc)], sib)
-
-    for t in range(2):
-        for q in along:
-            to_z(t, q).start()
-    for t in range(2):
-        for q in near:
-            to_plane(t, z, q).start()
-        to_sib(t, j, z).start()
-    for pz in along[::-1]:
-        for t in range(2):
-            arrived(t, j, pz, core).wait_recv()
-            for q in near:
-                to_plane(t, pz, q).start()
-            to_sib(t, j, pz).start()
     def finish(pz, pc):
         lo = pl.multiple_of((pc * nz + pz) * rz, rz)
-        held_pred = pred[pc * nz + pz]
+        held_pred = jnp.concatenate([pred[dev_of(q, pz, pc)] for q in range(gc)], axis=1)
         pred_out[pl.ds(lo, rz), :] = held_pred[:, :classes]
         fixes = jnp.zeros((16, 128), F32)
         for q in range(gc):
@@ -409,6 +408,7 @@
             for t in range(2):
                 arrived(t, q, pz, core).wait_recv()
                 to_sib(t, q, pz).start()
+    for pz in [z] + along[::-1]:
         finish(pz, core)
     out = apply(core)
     for pz in [z] + along[::-1]:
@@ -472,7 +472,7 @@
             pltpu.VMEM((rows_b, width), BF16),
             pltpu.VMEM((nz, rz, cs), F32),
             pltpu.VMEM((nz, rz, cs), F32),
-            pltpu.VMEM((CORES * nz, rz, gc * cs), BF16),
+            pltpu.VMEM((n, rz, cs), BF16),
             pltpu.VMEM((n, 16, 128), BF16),
             pltpu.VMEM((2 * held + 2 * sub_dev, rows_b), BF16),
             pltpu.VMEM((rows_b, gc * cs), BF16),

time: 53.6 us -> 53.6 us (level)
  no operation moved by 1% of the time
where the time goes in v4:
time: 53.6 us; the launch traced here: 53.4 us
  Pallas kernels  46.7 us (87%)
  local copies, waits for them, and re-layouts  6.06 us (11%)
  between operations  0.68 us (1%)
    pallas_call x1, Pallas kernels, fused(): pl.pallas_call(functools.partial(body, n_blk, n_grid, share), out_shape=(...  46.7 us
    unnamed x15, local copies, waits for them, and re-layouts  3.9 us
    pallas_call x2, local copies, waits for them, and re-layouts, fused(): pl.pallas_call(functools.partial(body, n_blk, n_grid, share), out_shape=(...  2.16 us

profile of v4, /device:TPU:1, one launch (start us, length us, event | category | flops | bytes accessed | tf_op | source)
XLA Modules:
  0.0 53.4 jit_solution(16501633063548604306)
XLA Ops:
  0.6 0.0 copy-start.4
  0.6 0.0 copy-start.2
  0.7 0.0 copy-start.3
  0.7 0.0 copy-start.5
  0.7 0.6 %copy-done.4 = s32[512]{0:T(512)S(1)} copy-done((s32[512]{0:T(512)S(1)}, s32[512]{0:T(512)}, u32[]{:S(2)}) %copy-start.4) | copy-done | bytes 2072
  1.3 0.0 copy-done.2
  1.3 0.0 copy-done.3
  1.3 0.0 copy-done.5
  1.4 0.0 copy-start
  1.4 1.0 %copy-done = f32[128,1000]{0,1:T(8,128)S(1)} copy-done((f32[128,1000]{0,1:T(8,128)S(1)}, f32[128,1000]{0,1:T(8,128)}, u32[]{:S(2)}) %copy-start) | copy-done | bytes 512024
  2.4 0.0 copy-start.1
  2.4 0.9 %copy-done.1 = bf16[128,512]{1,0:T(8,128)(2,1)S(1)} copy-done((bf16[128,512]{1,0:T(8,128)(2,1)S(1)}, bf16[128,512]{1,0:T(8,128)(2,1)}, u32[]{:S(2)}) %copy-start.1) | copy-done | bytes 131096
  3.3 0.0 copy-start.6
  3.3 0.7 %copy-done.6 = s32[8]{0:T(128)S(1)} copy-done((s32[8]{0:T(128)S(1)}, s32[8]{0:T(128)}, u32[]{:S(2)}) %copy-start.6) | copy-done | bytes 56
  4.0 46.7 %shard_map.94 = (bf16[512,1000]{1,0:T(8,128)(2,1)S(1)}, bf16[128,1000]{1,0:T(8,128)(2,1)S(1)}, f32[8,1000]{1,0:T(8,128)S(1)}) custom-call(bf16[128,512]{1,0:T(8,128)(2,1)S(1)} %copy-done.1, f32[1000,128]{1,0:T(8,128)S(1)} %bitcast.5, s32[1,512]{1,0:T(1,128)S(1)} %bitcast.6, s32[1,512]{1,0:T(1,128)S(1)} %bitcast.7, s32[1,8]{1,0:T(1,128)S(1)} %bitcast.9, ...), custom_call_target="tpu_custom_call" | custom-call | tf_op jit(solution)/shard_map/pallas_call | solution.py:457
  50.6 1.3 %copy.10 = bf16[512,1000]{0,1:T(8,128)(2,1)} copy(bf16[512,1000]{1,0:T(8,128)(2,1)S(1)} %get-tuple-element.3) | data formatting | bytes 2048000 | tf_op jit(solution)/shard_map/pallas_call | solution.py:457
  51.9 0.9 %copy.11 = bf16[128,1000]{0,1:T(8,128)(2,1)} copy(bf16[128,1000]{1,0:T(8,128)(2,1)S(1)} %get-tuple-element.4) | data formatting | bytes 512000 | tf_op jit(solution)/shard_map/pallas_call | solution.py:457
  52.8 0.6 %copy.13 = f32[8,1000]{1,0:T(8,128)} copy(f32[8,1000]{1,0:T(8,128)S(1)} %get-tuple-element.11) | data formatting | bytes 64000
Async XLA Ops:
  0.6 0.7 %copy-start.4 = (s32[512]{0:T(512)S(1)}, s32[512]{0:T(512)}, u32[]{:S(2)}) copy-start(s32[512]{0:T(512)} %param.10) | copy-start | bytes 6148
  0.6 0.7 %copy-start.2 = (bf16[8,160]{1,0:T(8,128)(2,1)S(1)}, bf16[8,160]{1,0:T(8,128)(2,1)}, u32[]{:S(2)}) copy-start(bf16[8,160]{1,0:T(8,128)(2,1)} %eigvecs.1) | copy-start | bytes 7684
  0.7 0.7 %copy-start.3 = (s32[512]{0:T(512)S(1)}, s32[512]{0:T(512)}, u32[]{:S(2)}) copy-start(s32[512]{0:T(512)} %param.9) | copy-start | bytes 6148
  0.7 0.7 %copy-start.5 = (f32[160]{0:T(256)S(1)}, f32[160]{0:T(256)}, u32[]{:S(2)}) copy-start(f32[160]{0:T(256)} %param.13) | copy-start | bytes 1924
  1.4 1.0 %copy-start = (f32[128,1000]{0,1:T(8,128)S(1)}, f32[128,1000]{0,1:T(8,128)}, u32[]{:S(2)}) copy-start(f32[128,1000]{0,1:T(8,128)} %param.8) | copy-start | bytes 1536004
  2.4 0.9 %copy-start.1 = (bf16[128,512]{1,0:T(8,128)(2,1)S(1)}, bf16[128,512]{1,0:T(8,128)(2,1)}, u32[]{:S(2)}) copy-start(bf16[128,512]{1,0:T(8,128)(2,1)} %centers.1) | copy-start | bytes 393220
  3.3 0.7 %copy-start.6 = (s32[8]{0:T(128)S(1)}, s32[8]{0:T(128)}, u32[]{:S(2)}) copy-start(s32[8]{0:T(128)} %param.11) | copy-start | bytes 100
